TPU v7x, 32 devices: a whole 2x2x4 slice. The times are simulated.
32 devices in a mesh: groups: 2 (over y), wide: 8 (over z, x), mp: 2 (over core).
Axes of the slice: x: 2, y: 2, z: 4, core: 2. Of those that a mesh axis runs over, the one named last changes fastest.
Arguments:
- queries: bfloat16 [2048, 5120], P(('groups', 'wide'), 'mp'), parts along dimension 0, may hold values from -40 to 40
- keys: bfloat16 [2048, 1024], P(('groups', 'wide'), 'mp'), parts along dimension 0, may hold values from -6 to 6
- values: bfloat16 [2048, 1024], P(('groups', 'wide'), 'mp'), parts along dimension 0, may hold values from -6 to 6
- prefix_keys: bfloat16 [2048, 1024], P(('groups', 'wide'), 'mp'), parts along dimension 0, may hold values from -6 to 6
- prefix_values: bfloat16 [2048, 1024], P(('groups', 'wide'), 'mp'), parts along dimension 0, may hold values from -6 to 6
- out_grad: bfloat16 [2048, 5120], P(('groups', 'wide'), 'mp'), parts along dimension 0, may hold values from -96 to 96
- row_prompt: int32 [2048, 1], P(('groups', 'wide')), parts along dimension 0, may hold values from 0 to 7; in each aligned block of 128 rows (0 to 127, 128 to 255, ...) at most 32 rows name the same one
Outputs:
- attn_out: bfloat16 [2048, 5120], P(('groups', 'wide'), 'mp'), parts along dimension 0
- query_grad: bfloat16 [2048, 5120], P(('groups', 'wide'), 'mp'), parts along dimension 0
- key_grad: bfloat16 [2048, 1024], P(('groups', 'wide'), 'mp'), parts along dimension 0
- value_grad: bfloat16 [2048, 1024], P(('groups', 'wide'), 'mp'), parts along dimension 0
- prefix_key_grad: bfloat16 [2048, 1024], P(('groups', 'wide'), 'mp'), parts along dimension 0
- prefix_value_grad: bfloat16 [2048, 1024], P(('groups', 'wide'), 'mp'), parts along dimension 0
There are 2 independent parts, one for each index of `groups`. A program takes and returns all parts, laid end to end along the dimension named above; each array names one. Nothing has to cross between parts.
Inputs may be any that keep to these rules, and one draw needn't show every extreme that they name: `row_prompt`: in every aligned block of 128 rows at most 32 rows name the same prompt, and in some block exactly 32 rows do.
All inputs are finite; a program needn't handle non-finite values.
Results may differ from a plain program's by a relative error of at most 0.024.
Values may be sent and summed in bfloat16 or wider, within the bound.
A program may use at most 128 MiB of HBM per device.

v0:
```python
import jax
import jax.numpy as jnp
from jax import lax
from jax.sharding import PartitionSpec as P

QH = 40
KH = 8
HD = 128


def part_forward(query_heads, key_rows, value_rows, allowed, score_scale):
    outputs, maxima, totals = ([], [], [])
    for head_group in range(query_heads.shape[1]):
        scores = (
            jnp.einsum(
                "rhd,kd->hrk",
                query_heads[:, head_group],
                key_rows[:, head_group],
                preferred_element_type=jnp.float32,
            )
            * score_scale
        )
        if allowed is not None:
            scores = jnp.where(allowed[None], scores, -jnp.inf)
        row_max = jnp.max(scores, axis=2)
        weights = jnp.exp(scores - row_max[:, :, None])
        totals.append(jnp.sum(weights, axis=2))
        maxima.append(row_max)
        outputs.append(
            jnp.einsum(
                "hrk,kd->rhd",
                weights.astype(jnp.bfloat16),
                value_rows[:, head_group],
                preferred_element_type=jnp.float32,
            )
        )
    row_count = query_heads.shape[0]
    partial_value = jnp.stack(outputs, axis=1).reshape(row_count, -1)
    return (partial_value, jnp.concatenate(maxima, axis=0).T, jnp.concatenate(totals, axis=0).T)


def part_backward(
    query_heads, key_rows, value_rows, allowed, score_scale, grad_heads, log_total, row_delta
):
    group_size = query_heads.shape[2]
    query_parts, key_parts, value_parts = ([], [], [])
    for head_group in range(query_heads.shape[1]):
        first = head_group * group_size
        query_block = query_heads[:, head_group]
        key_block = key_rows[:, head_group]
        value_block = value_rows[:, head_group]
        grad_block = grad_heads[:, head_group]
        scores = (
            jnp.einsum("rhd,kd->hrk", query_block, key_block, preferred_element_type=jnp.float32)
            * score_scale
        )
        if allowed is not None:
            scores = jnp.where(allowed[None], scores, -jnp.inf)
        group_total = log_total[:, first : first + group_size].T
        group_delta = row_delta[:, first : first + group_size].T
        probs = jnp.exp(scores - group_total[:, :, None])
        value_parts.append(
            jnp.einsum(
                "hrk,rhd->kd",
                probs.astype(jnp.bfloat16),
                grad_block,
                preferred_element_type=jnp.float32,
            )
        )
        dprob = jnp.einsum(
            "rhd,kd->hrk", grad_block, value_block, preferred_element_type=jnp.float32
        )
        dscore = (probs * (dprob - group_delta[:, :, None])).astype(jnp.bfloat16)
        query_parts.append(
            jnp.einsum("hrk,kd->rhd", dscore, key_block, preferred_element_type=jnp.float32)
            * score_scale
        )
        key_parts.append(
            jnp.einsum("hrk,rhd->kd", dscore, query_block, preferred_element_type=jnp.float32)
            * score_scale
        )
    row_count = query_heads.shape[0]
    key_count = key_rows.shape[0]
    return (
        jnp.stack(query_parts, axis=1).reshape(row_count, -1),
        jnp.stack(key_parts, axis=1).reshape(key_count, -1),
        jnp.stack(value_parts, axis=1).reshape(key_count, -1),
    )


def merge_parts(first_out, first_max, first_total, second_out, second_max, second_total, head_size):
    joint_max = jnp.maximum(first_max, second_max)
    first_factor = jnp.exp(first_max - joint_max)
    second_factor = jnp.exp(second_max - joint_max)
    joint_total = first_factor * first_total + second_factor * second_total
    row_count, head_count = first_max.shape
    combined = (
        first_out.reshape(row_count, head_count, head_size) * first_factor[:, :, None]
        + second_out.reshape(row_count, head_count, head_size) * second_factor[:, :, None]
    ) / joint_total[:, :, None]
    return (
        combined.reshape(row_count, head_count * head_size).astype(jnp.bfloat16),
        joint_max + jnp.log(joint_total),
    )


def out_delta(grad_rows, out_rows, head_size):
    row_count = grad_rows.shape[0]
    product = grad_rows.astype(jnp.float32) * out_rows.astype(jnp.float32)
    return jnp.sum(product.reshape(row_count, -1, head_size), axis=2)


def per_device(queries, keys, values, prefix_keys, prefix_values, out_grad, row_prompt):
    tok_rows = queries.shape[0]
    n_wide = lax.axis_size("wide")
    capacity = 2 * tok_rows // n_wide
    slot_total = n_wide * capacity
    kv_count = keys.shape[1] // HD
    group_size = QH // KH
    prefix_rows = prefix_keys.shape[0]
    score_scale = HD ** (-0.5)
    prompt = row_prompt[:, 0]
    positions = jnp.arange(tok_rows, dtype=jnp.int32)
    owner_hits = prompt[:, None] == jnp.arange(n_wide, dtype=jnp.int32)[None, :]
    earlier = (positions[None, :] < positions[:, None]).astype(jnp.bfloat16)
    seen_before = jnp.dot(
        earlier, owner_hits.astype(jnp.bfloat16), preferred_element_type=jnp.float32
    )
    row_rank = jnp.sum(jnp.where(owner_hits, seen_before, 0.0), axis=1).astype(jnp.int32)
    slot_index = prompt * capacity + row_rank
    allowed = (prompt[:, None] == prompt[None, :]) & (positions[None, :] <= positions[:, None])
    query_heads = queries.reshape(tok_rows, kv_count, group_size, HD)
    key_heads = keys.reshape(tok_rows, kv_count, HD)
    value_heads = values.reshape(tok_rows, kv_count, HD)
    grad_heads = out_grad.reshape(tok_rows, kv_count, group_size, HD)
    prefix_key_heads = prefix_keys.reshape(prefix_rows, kv_count, HD)
    prefix_value_heads = prefix_values.reshape(prefix_rows, kv_count, HD)

    def to_slots(row_array):
        return (
            jnp.zeros((slot_total,) + row_array.shape[1:], row_array.dtype)
            .at[slot_index]
            .set(row_array)
        )

    def from_slots(slot_array):
        return slot_array[slot_index]

    def slot_heads(slot_array):
        return slot_array.reshape(slot_total, kv_count, group_size, HD)

    own_out, own_max, own_total = part_forward(
        query_heads, key_heads, value_heads, allowed, score_scale
    )
    sent_queries = lax.all_to_all(
        to_slots(queries), "wide", split_axis=0, concat_axis=0, tiled=True
    )
    owner_queries = slot_heads(sent_queries)
    prefix_out, prefix_max, prefix_total = part_forward(
        owner_queries, prefix_key_heads, prefix_value_heads, None, score_scale
    )
    returned_out, returned_max, returned_total = (
        lax.all_to_all(prefix_out, "wide", split_axis=0, concat_axis=0, tiled=True),
        lax.all_to_all(prefix_max, "wide", split_axis=0, concat_axis=0, tiled=True),
        lax.all_to_all(prefix_total, "wide", split_axis=0, concat_axis=0, tiled=True),
    )
    attn_out, log_total = merge_parts(
        from_slots(returned_out),
        from_slots(returned_max),
        from_slots(returned_total),
        own_out,
        own_max,
        own_total,
        HD,
    )
    row_delta = out_delta(out_grad, attn_out, HD)
    arrived_grad, arrived_total, arrived_delta = (
        lax.all_to_all(
            to_slots(out_grad).astype(jnp.float32), "wide", split_axis=0, concat_axis=0, tiled=True
        ).astype(jnp.bfloat16),
        lax.all_to_all(to_slots(log_total), "wide", split_axis=0, concat_axis=0, tiled=True),
        lax.all_to_all(to_slots(row_delta), "wide", split_axis=0, concat_axis=0, tiled=True),
    )
    prefix_query, prefix_key, prefix_value = part_backward(
        owner_queries,
        prefix_key_heads,
        prefix_value_heads,
        None,
        score_scale,
        slot_heads(arrived_grad),
        arrived_total,
        arrived_delta,
    )
    returned_query = lax.all_to_all(
        prefix_query.astype(jnp.bfloat16), "wide", split_axis=0, concat_axis=0, tiled=True
    )
    prefix_query_rows = from_slots(returned_query)
    own_query, own_key, own_value = part_backward(
        query_heads, key_heads, value_heads, allowed, score_scale, grad_heads, log_total, row_delta
    )
    query_grad = (prefix_query_rows.astype(jnp.float32) + own_query).astype(jnp.bfloat16)
    return (
        attn_out,
        query_grad,
        own_key.astype(jnp.bfloat16),
        own_value.astype(jnp.bfloat16),
        prefix_key.astype(jnp.bfloat16),
        prefix_value.astype(jnp.bfloat16),
    )


def solution(mesh):
    in_specs = (
        P(("groups", "wide"), "mp"),
        P(("groups", "wide"), "mp"),
        P(("groups", "wide"), "mp"),
        P(("groups", "wide"), "mp"),
        P(("groups", "wide"), "mp"),
        P(("groups", "wide"), "mp"),
        P(("groups", "wide"), None),
    )
    out_specs = (
        P(("groups", "wide"), "mp"),
        P(("groups", "wide"), "mp"),
        P(("groups", "wide"), "mp"),
        P(("groups", "wide"), "mp"),
        P(("groups", "wide"), "mp"),
        P(("groups", "wide"), "mp"),
    )
    return jax.shard_map(
        per_device, mesh=mesh, in_specs=in_specs, out_specs=out_specs, check_vma=False
    )
```

profile of v0, /device:TPU:0, one launch (start us, length us, event | category | flops | bytes accessed | tf_op | source)
XLA Modules:
  0.0 253.9 jit_solution(11321886146899608750)
XLA Ops:
  2.2 3.3 %scatter_custom_fusion = bf16[256,2560]{1,0:T(8,128)(2,1)} fusion(s32[128]{0:T(128)S(1)} %fusion.158, bf16[128,2560]{1,0:T(8,128)(2,1)} %param.7, bf16[]{:T(256)} %constant.7.clone.1), kind=kCustom, calls=%fused_computation.163 | custom fusion | bytes 1311232 | tf_op jit(solution)/shard_map/scatter | solution.py:143
  5.5 7.4 %all-to-all-start = ((bf16[8,32,2560]{2,1,0:T(8,128)(2,1)}), bf16[8,32,2560]{2,1,0:T(8,128)(2,1)}, u32[]{:S(2)}, u32[]{:S(2)}) async-start(bf16[8,32,2560]{2,1,0:T(8,128)(2,1)} %bitcast.3), calls=%async_computation | async-start | bytes 2621440 | tf_op jit(solution)/shard_map/all_to_all | solution.py:155
  13.0 31.4 %all-to-all-done = bf16[8,32,2560]{2,1,0:T(8,128)(2,1)} async-done(((bf16[8,32,2560]{2,1,0:T(8,128)(2,1)}), bf16[8,32,2560]{2,1,0:T(8,128)(2,1)}, u32[]{:S(2)}, u32[]{:S(2)}) %all-to-all-start) | async-done | bytes 1310752 | tf_op jit(solution)/shard_map/all_to_all | solution.py:155
  44.4 3.1 %reshape.159 = bf16[256,4,5,128]{3,2,1,0:T(8,128)(2,1)S(1)} reshape(bf16[8,32,2560]{2,1,0:T(8,128)(2,1)} %all-to-all-done) | data formatting | bytes 2621440 | tf_op jit(solution)/shard_map/reshape | solution.py:150
  50.4 3.6 %all-to-all-start.2 = ((f32[8,1,640]{2,1,0:T(1,128)}), f32[8,1,640]{2,1,0:T(1,128)S(1)}, u32[]{:S(2)}, u32[]{:S(2)}) async-start(f32[8,1,640]{2,1,0:T(1,128)} %reshape.281), calls=%async_computation.2 | async-start | bytes 40960 | tf_op jit(solution)/shard_map/all_to_all | solution.py:164
  55.3 5.3 %all-to-all-done.2 = f32[8,1,640]{2,1,0:T(1,128)S(1)} async-done(((f32[8,1,640]{2,1,0:T(1,128)}), f32[8,1,640]{2,1,0:T(1,128)S(1)}, u32[]{:S(2)}, u32[]{:S(2)}) %all-to-all-start.2) | async-done | bytes 20512 | tf_op jit(solution)/shard_map/all_to_all | solution.py:164
  60.7 3.3 %all-to-all-start.3 = ((f32[8,1,640]{2,1,0:T(1,128)}), f32[8,1,640]{2,1,0:T(1,128)S(1)}, u32[]{:S(2)}, u32[]{:S(2)}) async-start(f32[8,1,640]{2,1,0:T(1,128)} %reshape.283), calls=%async_computation.3 | async-start | bytes 40960 | tf_op jit(solution)/shard_map/all_to_all | solution.py:165
  64.0 3.4 %scatter_custom_fusion.2 = bf16[256,2560]{1,0:T(8,128)(2,1)} fusion(s32[128]{0:T(128)S(1)} %fusion.158, bf16[128,2560]{1,0:T(8,128)(2,1)} %param.12, bf16[]{:T(256)} %constant.7.clone.1), kind=kCustom, calls=%fused_computation.161 | custom fusion | bytes 1311232 | tf_op jit(solution)/shard_map/scatter | solution.py:143
  67.4 3.1 %all-to-all-done.3 = f32[8,1,640]{2,1,0:T(1,128)S(1)} async-done(((f32[8,1,640]{2,1,0:T(1,128)}), f32[8,1,640]{2,1,0:T(1,128)S(1)}, u32[]{:S(2)}, u32[]{:S(2)}) %all-to-all-start.3) | async-done | bytes 20512 | tf_op jit(solution)/shard_map/all_to_all | solution.py:165
  71.1 4.3 %all-to-all-start.5 = ((bf16[8,32,2560]{2,1,0:T(8,128)(2,1)}), bf16[8,32,2560]{2,1,0:T(8,128)(2,1)}, u32[]{:S(2)}, u32[]{:S(2)}) async-start(bf16[8,32,2560]{2,1,0:T(8,128)(2,1)} %bitcast.671), calls=%async_computation.5 | async-start | bytes 2621440 | tf_op jit(solution)/shard_map/all_to_all | solution.py:178
  76.0 1.4 copy.480
  93.2 11.7 %all-to-all-done.5 = bf16[8,32,2560]{2,1,0:T(8,128)(2,1)} async-done(((bf16[8,32,2560]{2,1,0:T(8,128)(2,1)}), bf16[8,32,2560]{2,1,0:T(8,128)(2,1)}, u32[]{:S(2)}, u32[]{:S(2)}) %all-to-all-start.5) | async-done | bytes 1310752 | tf_op jit(solution)/shard_map/all_to_all | solution.py:178
  104.9 3.5 %all-to-all-start.4 = ((f32[8,1,640]{2,1,0:T(1,128)}), f32[8,1,640]{2,1,0:T(1,128)S(1)}, u32[]{:S(2)}, u32[]{:S(2)}) async-start(f32[8,1,640]{2,1,0:T(1,128)} %reshape.287), calls=%async_computation.4 | async-start | bytes 40960 | tf_op jit(solution)/shard_map/all_to_all | solution.py:181
  108.4 1.3 pad_maximum_fusion
  109.7 3.5 %copy.475 = f32[256,4,5,128]{3,2,1,0:T(8,128)} copy(f32[256,4,5,128]{3,0,2,1:T(8,128)S(1)} %pad_maximum_fusion) | data formatting | bytes 5242880 | tf_op jit(solution)/shard_map/stack | solution.py:38
  113.3 4.7 %all_to_all.62 = f32[8,32,2560]{2,1,0:T(8,128)} reshape(f32[256,4,5,128]{3,2,1,0:T(8,128)} %copy.475) | data formatting | bytes 5242880 | tf_op jit(solution)/shard_map/all_to_all | solution.py:163
  118.6 5.9 %all-to-all-start.1 = ((f32[8,32,2560]{2,1,0:T(8,128)}), f32[8,32,2560]{2,1,0:T(8,128)S(1)}, u32[]{:S(2)}, u32[]{:S(2)}) async-start(f32[8,32,2560]{2,1,0:T(8,128)} %all_to_all.62), calls=%async_computation.1 | async-start | bytes 5242880 | tf_op jit(solution)/shard_map/all_to_all | solution.py:163
  124.5 2.2 copy.522
  127.7 1.3 convolution_bitcast_fusion.8
  131.8 2.8 %copy.496 = f32[128,2560]{1,0:T(8,128)} copy(f32[128,2560]{0,1:T(8,128)} %bitcast.672) | data formatting | bytes 2621440 | tf_op jit(solution)/shard_map/reshape;reshape | solution.py:99
  134.6 4.1 %convert_element_type.143 = bf16[256,4,5,128]{3,2,1,0:T(8,128)(2,1)} reshape(bf16[8,32,2560]{2,1,0:T(8,128)(2,1)} %all-to-all-done.5) | data formatting | bytes 2621440 | tf_op jit(solution)/shard_map/convert_element_type | solution.py:180
  138.8 3.1 %fusion.160 = (bf16[256,1,5,128]{3,2,1,0:T(8,128)(2,1)}, bf16[256,1,5,128]{3,2,1,0:T(8,128)(2,1)}, bf16[256,1,5,128]{3,2,1,0:T(8,128)(2,1)}, bf16[256,1,5,128]{3,2,1,0:T(8,128)(2,1)}) fusion(bf16[256,4,5,128]{3,2,1,0:T(8,128)(2,1)} %convert_element_type.143), kind=kLoop, calls=%fused_computation.288 | loop fusion | bytes 2621440 | tf_op jit(solution)/shard_map/slice | solution.py:52
  143.1 2.8 %copy.501 = f32[128,2560]{1,0:T(8,128)} copy(f32[128,2560]{0,1:T(8,128)} %bitcast.674) | data formatting | bytes 2621440 | tf_op jit(solution)/shard_map/div | solution.py:97
  147.0 2.8 %copy.497 = f32[128,2560]{1,0:T(8,128)} copy(f32[128,2560]{0,1:T(8,128)} %bitcast.675) | data formatting | bytes 2621440 | tf_op jit(solution)/shard_map/mul | solution.py:99
  151.0 2.8 %copy.490 = f32[128,2560]{1,0:T(8,128)} copy(f32[128,2560]{0,1:T(8,128)} %bitcast.676) | data formatting | bytes 2621440 | tf_op jit(solution)/shard_map/mul | solution.py:98
  153.8 1.3 fusion.80
  155.1 1.2 fusion.81
  156.3 1.2 fusion.82
  159.5 1.4 reduce.3
  162.7 1.7 fusion.72
  164.4 1.6 fusion.73
  167.5 16.1 %all-to-all-done.1 = f32[8,32,2560]{2,1,0:T(8,128)S(1)} async-done(((f32[8,32,2560]{2,1,0:T(8,128)}), f32[8,32,2560]{2,1,0:T(8,128)S(1)}, u32[]{:S(2)}, u32[]{:S(2)}) %all-to-all-start.1) | async-done | bytes 2621472 | tf_op jit(solution)/shard_map/all_to_all | solution.py:163
  183.6 2.2 gather_fusion
  185.8 4.6 %convert_multiply_fusion = (f32[128,2560]{1,0:T(8,128)S(1)}, bf16[128,2560]{1,0:T(8,128)(2,1)}) fusion(bf16[128,2560]{1,0:T(8,128)(2,1)} %param.12, f32[128,2560]{1,0:T(8,128)} %copy.501, f32[128,2560]{1,0:T(8,128)} %copy.496, f32[128,2560]{1,0:T(8,128)} %copy.497, f32[128,2560]{1,0:T(8,128)} %gather_fusion, f32[128,2560]{1,0:T(8,128)} %copy.490), kind=kLoop, calls=%fused_computation.13 | loop fusion | flops 2621440 | bytes 9175040 | tf_op jit(solution)/shard_map/mul | solution.py:109
  190.3 1.5 copy.507
  191.9 1.5 reduce_sum.99
  197.2 3.6 %all-to-all-start.6 = ((f32[8,1,640]{2,1,0:T(1,128)}), f32[8,1,640]{2,1,0:T(1,128)S(1)}, u32[]{:S(2)}, u32[]{:S(2)}) async-start(f32[8,1,640]{2,1,0:T(1,128)} %reshape.285), calls=%async_computation.6 | async-start | bytes 40960 | tf_op jit(solution)/shard_map/all_to_all | solution.py:182
  201.8 5.7 %all-to-all-done.6 = f32[8,1,640]{2,1,0:T(1,128)S(1)} async-done(((f32[8,1,640]{2,1,0:T(1,128)}), f32[8,1,640]{2,1,0:T(1,128)S(1)}, u32[]{:S(2)}, u32[]{:S(2)}) %all-to-all-start.6) | async-done | bytes 20512 | tf_op jit(solution)/shard_map/all_to_all | solution.py:182
  208.4 1.3 fusion.15
  210.1 1.5 fusion.14
  215.3 2.3 convert_element_type.150
  217.6 3.7 %all-to-all-start.7 = ((bf16[8,32,2560]{2,1,0:T(8,128)(2,1)}), bf16[8,32,2560]{2,1,0:T(8,128)(2,1)S(1)}, u32[]{:S(2)}, u32[]{:S(2)}) async-start(bf16[8,32,2560]{2,1,0:T(8,128)(2,1)} %convert_element_type.150), calls=%async_computation.7 | async-start | bytes 2621440 | tf_op jit(solution)/shard_map/all_to_all | solution.py:194
  223.9 1.8 copy.539
  230.1 1.4 fusion.76
  231.6 1.5 fusion.77
  233.1 1.5 fusion.78
  234.5 1.3 fusion.79
  236.7 15.2 %all-to-all-done.7 = bf16[8,32,2560]{2,1,0:T(8,128)(2,1)S(1)} async-done(((bf16[8,32,2560]{2,1,0:T(8,128)(2,1)}), bf16[8,32,2560]{2,1,0:T(8,128)(2,1)S(1)}, u32[]{:S(2)}, u32[]{:S(2)}) %all-to-all-start.7) | async-done | bytes 1310752 | tf_op jit(solution)/shard_map/all_to_all | solution.py:194
  (288 shorter events, 54.3 us)
Async XLA Ops:
  2.2 73.2 %copy-start.90 = (s32[128]{0:T(128)}, s32[128]{0:T(128)S(1)}, u32[]{:S(2)}) copy-start(s32[128]{0:T(128)S(1)} %fusion.158) | copy-start | bytes 1540
  5.5 7.4 %copy-start.53 = (bf16[128,512]{1,0:T(8,128)(2,1)S(1)}, bf16[128,512]{1,0:T(8,128)(2,1)}, u32[]{:S(2)}) copy-start(bf16[128,512]{1,0:T(8,128)(2,1)} %param.10) | copy-start | bytes 393220
  5.5 38.9 %all-to-all-start = ((bf16[8,32,2560]{2,1,0:T(8,128)(2,1)}), bf16[8,32,2560]{2,1,0:T(8,128)(2,1)}, u32[]{:S(2)}, u32[]{:S(2)}) async-start(bf16[8,32,2560]{2,1,0:T(8,128)(2,1)} %bitcast.3), calls=%async_computation | async-start | bytes 2621440 | tf_op jit(solution)/shard_map/all_to_all | solution.py:155
  13.0 36.1 %copy-start.42 = (bf16[128,512]{0,1:T(8,128)(2,1)}, bf16[128,512]{0,1:T(8,128)(2,1)S(1)}, u32[]{:S(2)}) copy-start(bf16[128,512]{0,1:T(8,128)(2,1)S(1)} %copy.458) | copy-start | bytes 393220
  48.3 34.2 %copy-start.5 = (f32[5,256,128]{1,2,0:T(8,128)}, f32[5,256,128]{1,2,0:T(8,128)S(1)}, u32[]{:S(2)}) copy-start(f32[5,256,128]{1,2,0:T(8,128)S(1)} %get-tuple-element.67) | copy-start | bytes 1966084
  48.6 34.2 %copy-start.3 = (f32[5,256,128]{1,2,0:T(8,128)}, f32[5,256,128]{1,2,0:T(8,128)S(1)}, u32[]{:S(2)}) copy-start(f32[5,256,128]{1,2,0:T(8,128)S(1)} %get-tuple-element.69) | copy-start | bytes 1966084
  49.1 5.2 %copy-start.49 = (f32[5,256]{1,0:T(8,128)}, f32[5,256]{1,0:T(8,128)S(1)}, u32[]{:S(2)}) copy-start(f32[5,256]{1,0:T(8,128)S(1)} %get-tuple-element.70) | copy-start | bytes 15364
  49.1 34.9 %copy-start = (f32[5,256,128]{1,2,0:T(8,128)}, f32[5,256,128]{1,2,0:T(8,128)S(1)}, u32[]{:S(2)}) copy-start(f32[5,256,128]{1,2,0:T(8,128)S(1)} %get-tuple-element.71) | copy-start | bytes 1966084
  49.6 4.9 %copy-start.51 = (f32[5,256]{1,0:T(8,128)}, f32[5,256]{1,0:T(8,128)S(1)}, u32[]{:S(2)}) copy-start(f32[5,256]{1,0:T(8,128)S(1)} %get-tuple-element.72) | copy-start | bytes 15364
  50.4 10.2 %all-to-all-start.2 = ((f32[8,1,640]{2,1,0:T(1,128)}), f32[8,1,640]{2,1,0:T(1,128)S(1)}, u32[]{:S(2)}, u32[]{:S(2)}) async-start(f32[8,1,640]{2,1,0:T(1,128)} %reshape.281), calls=%async_computation.2 | async-start | bytes 40960 | tf_op jit(solution)/shard_map/all_to_all | solution.py:164
  60.7 9.9 %copy-start.55 = (f32[8,1,640]{2,1,0:T(1,128)}, f32[8,1,640]{2,1,0:T(1,128)S(1)}, u32[]{:S(2)}) copy-start(f32[8,1,640]{2,1,0:T(1,128)S(1)} %all-to-all-done.2) | copy-start | bytes 61444
  60.7 9.9 %all-to-all-start.3 = ((f32[8,1,640]{2,1,0:T(1,128)}), f32[8,1,640]{2,1,0:T(1,128)S(1)}, u32[]{:S(2)}, u32[]{:S(2)}) async-start(f32[8,1,640]{2,1,0:T(1,128)} %reshape.283), calls=%async_computation.3 | async-start | bytes 40960 | tf_op jit(solution)/shard_map/all_to_all | solution.py:165
  71.1 33.7 %all-to-all-start.5 = ((bf16[8,32,2560]{2,1,0:T(8,128)(2,1)}), bf16[8,32,2560]{2,1,0:T(8,128)(2,1)}, u32[]{:S(2)}, u32[]{:S(2)}) async-start(bf16[8,32,2560]{2,1,0:T(8,128)(2,1)} %bitcast.671), calls=%async_computation.5 | async-start | bytes 2621440 | tf_op jit(solution)/shard_map/all_to_all | solution.py:178
  77.5 4.0 %copy-start.18 = (bf16[128,2560]{0,1:T(8,128)(2,1)}, bf16[128,2560]{0,1:T(8,128)(2,1)S(1)}, u32[]{:S(2)}) copy-start(bf16[128,2560]{0,1:T(8,128)(2,1)S(1)} %copy.480) | copy-start | bytes 1966084
  78.7 6.4 %copy-start.47 = (bf16[128,512]{0,1:T(8,128)(2,1)}, bf16[128,512]{0,1:T(8,128)(2,1)S(1)}, u32[]{:S(2)}) copy-start(bf16[128,512]{0,1:T(8,128)(2,1)S(1)} %copy.460) | copy-start | bytes 393220
  85.1 3.6 %copy-start.59 = (f32[8,1,640]{2,1,0:T(1,128)S(1)}, f32[8,1,640]{2,1,0:T(1,128)}, u32[]{:S(2)}) copy-start(f32[8,1,640]{2,1,0:T(1,128)} %copy-done.58) | copy-start | bytes 61444
  86.3 4.2 %copy-start.64 = (f32[5,128]{1,0:T(8,128)S(1)}, f32[5,128]{1,0:T(8,128)}, u32[]{:S(2)}) copy-start(f32[5,128]{1,0:T(8,128)} %copy-done.63) | copy-start | bytes 7684
  86.3 4.2 %copy-start.66 = (f32[5,128]{1,0:T(8,128)S(1)}, f32[5,128]{1,0:T(8,128)}, u32[]{:S(2)}) copy-start(f32[5,128]{1,0:T(8,128)} %copy-done.65) | copy-start | bytes 7684
  86.3 4.3 %copy-start.68 = (f32[5,128]{1,0:T(8,128)S(1)}, f32[5,128]{1,0:T(8,128)}, u32[]{:S(2)}) copy-start(f32[5,128]{1,0:T(8,128)} %copy-done.67) | copy-start | bytes 7684
  86.3 4.3 %copy-start.71 = (f32[5,128]{1,0:T(8,128)S(1)}, f32[5,128]{1,0:T(8,128)}, u32[]{:S(2)}) copy-start(f32[5,128]{1,0:T(8,128)} %copy-done.70) | copy-start | bytes 7684
  86.3 4.3 %copy-start.86 = (f32[5,128]{1,0:T(8,128)S(1)}, f32[5,128]{1,0:T(8,128)}, u32[]{:S(2)}) copy-start(f32[5,128]{1,0:T(8,128)} %get-tuple-element.88) | copy-start | bytes 7684
  86.3 4.3 %copy-start.87 = (f32[5,128]{1,0:T(8,128)S(1)}, f32[5,128]{1,0:T(8,128)}, u32[]{:S(2)}) copy-start(f32[5,128]{1,0:T(8,128)} %get-tuple-element.89) | copy-start | bytes 7684
  86.3 4.3 %copy-start.88 = (f32[5,128]{1,0:T(8,128)S(1)}, f32[5,128]{1,0:T(8,128)}, u32[]{:S(2)}) copy-start(f32[5,128]{1,0:T(8,128)} %get-tuple-element.86) | copy-start | bytes 7684
  86.3 4.3 %copy-start.89 = (f32[5,128]{1,0:T(8,128)S(1)}, f32[5,128]{1,0:T(8,128)}, u32[]{:S(2)}) copy-start(f32[5,128]{1,0:T(8,128)} %get-tuple-element.87) | copy-start | bytes 7684
  87.6 20.8 %copy-start.34 = (f32[256,1,5,128]{3,0,2,1:T(8,128)S(1)}, f32[256,1,5,128]{3,0,2,1:T(8,128)}, u32[]{:S(2)}) copy-start(f32[256,1,5,128]{3,0,2,1:T(8,128)} %convolution_bitcast_fusion.5) | copy-start | bytes 1966084
  87.6 20.8 %copy-start.35 = (f32[256,1,5,128]{3,0,2,1:T(8,128)S(1)}, f32[256,1,5,128]{3,0,2,1:T(8,128)}, u32[]{:S(2)}) copy-start(f32[256,1,5,128]{3,0,2,1:T(8,128)} %convolution_bitcast_fusion.6) | copy-start | bytes 1966084
  104.9 13.1 %all-to-all-start.4 = ((f32[8,1,640]{2,1,0:T(1,128)}), f32[8,1,640]{2,1,0:T(1,128)S(1)}, u32[]{:S(2)}, u32[]{:S(2)}) async-start(f32[8,1,640]{2,1,0:T(1,128)} %reshape.287), calls=%async_computation.4 | async-start | bytes 40960 | tf_op jit(solution)/shard_map/all_to_all | solution.py:181
  118.6 65.0 %all-to-all-start.1 = ((f32[8,32,2560]{2,1,0:T(8,128)}), f32[8,32,2560]{2,1,0:T(8,128)S(1)}, u32[]{:S(2)}, u32[]{:S(2)}) async-start(f32[8,32,2560]{2,1,0:T(8,128)} %all_to_all.62), calls=%async_computation.1 | async-start | bytes 5242880 | tf_op jit(solution)/shard_map/all_to_all | solution.py:163
  153.8 3.8 %copy-start.9 = (f32[5,128,128]{1,2,0:T(8,128)S(1)}, f32[5,128,128]{1,2,0:T(8,128)}, u32[]{:S(2)}) copy-start(f32[5,128,128]{1,2,0:T(8,128)} %copy-done.7) | copy-start | bytes 983044
  153.8 3.8 %copy-start.76 = (f32[5,128]{1,0:T(8,128)}, f32[5,128]{1,0:T(8,128)S(1)}, u32[]{:S(2)}) copy-start(f32[5,128]{1,0:T(8,128)S(1)} %get-tuple-element.58) | copy-start | bytes 7684
  153.8 3.8 %copy-start.78 = (f32[5,128]{1,0:T(8,128)}, f32[5,128]{1,0:T(8,128)S(1)}, u32[]{:S(2)}) copy-start(f32[5,128]{1,0:T(8,128)S(1)} %get-tuple-element.61) | copy-start | bytes 7684
  153.8 3.8 %copy-start.80 = (f32[5,128]{1,0:T(8,128)}, f32[5,128]{1,0:T(8,128)S(1)}, u32[]{:S(2)}) copy-start(f32[5,128]{1,0:T(8,128)S(1)} %get-tuple-element.60) | copy-start | bytes 7684
  153.8 3.8 %copy-start.82 = (f32[5,128]{1,0:T(8,128)}, f32[5,128]{1,0:T(8,128)S(1)}, u32[]{:S(2)}) copy-start(f32[5,128]{1,0:T(8,128)S(1)} %get-tuple-element.59) | copy-start | bytes 7684
  162.7 3.6 %copy-start.60 = (f32[5,256]{1,0:T(8,128)}, f32[5,256]{1,0:T(8,128)S(1)}, u32[]{:S(2)}) copy-start(f32[5,256]{1,0:T(8,128)S(1)} %get-tuple-element.52) | copy-start | bytes 15364
  190.3 3.8 %copy-start.45 = (bf16[128,512]{0,1:T(8,128)(2,1)S(1)}, bf16[128,512]{0,1:T(8,128)(2,1)}, u32[]{:S(2)}) copy-start(bf16[128,512]{0,1:T(8,128)(2,1)} %copy-done.44) | copy-start | bytes 393220
  194.1 14.2 %copy-start.6 = (f32[5,256,128]{1,2,0:T(8,128)S(1)}, f32[5,256,128]{1,2,0:T(8,128)}, u32[]{:S(2)}) copy-start(f32[5,256,128]{1,2,0:T(8,128)} %copy-done.5) | copy-start | bytes 1966084
  194.1 14.2 %copy-start.62 = (f32[5,256]{1,0:T(8,128)S(1)}, f32[5,256]{1,0:T(8,128)}, u32[]{:S(2)}) copy-start(f32[5,256]{1,0:T(8,128)} %copy-done.61) | copy-start | bytes 15364
  194.4 14.0 %copy-start.36 = (bf16[5,128,128]{1,2,0:T(8,128)(2,1)}, bf16[5,128,128]{1,2,0:T(8,128)(2,1)S(1)}, u32[]{:S(2)}) copy-start(bf16[5,128,128]{1,2,0:T(8,128)(2,1)S(1)} %fusion.47) | copy-start | bytes 491524
  196.5 13.2 %copy-start.43 = (bf16[128,512]{0,1:T(8,128)(2,1)S(1)}, bf16[128,512]{0,1:T(8,128)(2,1)}, u32[]{:S(2)}) copy-start(bf16[128,512]{0,1:T(8,128)(2,1)} %copy-done.42) | copy-start | bytes 393220
  197.2 10.2 %all-to-all-start.6 = ((f32[8,1,640]{2,1,0:T(1,128)}), f32[8,1,640]{2,1,0:T(1,128)S(1)}, u32[]{:S(2)}, u32[]{:S(2)}) async-start(f32[8,1,640]{2,1,0:T(1,128)} %reshape.285), calls=%async_computation.6 | async-start | bytes 40960 | tf_op jit(solution)/shard_map/all_to_all | solution.py:182
  201.8 8.3 %copy-start.4 = (f32[5,256,128]{1,2,0:T(8,128)S(1)}, f32[5,256,128]{1,2,0:T(8,128)}, u32[]{:S(2)}) copy-start(f32[5,256,128]{1,2,0:T(8,128)} %copy-done.3) | copy-start | bytes 1966084
  217.6 3.7 %copy-start.38 = (bf16[5,128,128]{1,2,0:T(8,128)(2,1)S(1)}, bf16[5,128,128]{1,2,0:T(8,128)(2,1)}, u32[]{:S(2)}) copy-start(bf16[5,128,128]{1,2,0:T(8,128)(2,1)} %fusion.46) | copy-start | bytes 491524
  217.6 4.0 %copy-start.13 = (f32[5,128,128]{1,2,0:T(8,128)S(1)}, f32[5,128,128]{1,2,0:T(8,128)}, u32[]{:S(2)}) copy-start(f32[5,128,128]{1,2,0:T(8,128)} %copy-done.11) | copy-start | bytes 983044
  217.6 4.0 %copy-start.46 = (bf16[128,512]{0,1:T(8,128)(2,1)S(1)}, bf16[128,512]{0,1:T(8,128)(2,1)}, u32[]{:S(2)}) copy-start(bf16[128,512]{0,1:T(8,128)(2,1)} %copy-done.44) | copy-start | bytes 393220
  217.6 4.0 %copy-start.79 = (f32[5,128]{1,0:T(8,128)S(1)}, f32[5,128]{1,0:T(8,128)}, u32[]{:S(2)}) copy-start(f32[5,128]{1,0:T(8,128)} %copy-done.78) | copy-start | bytes 7684
  217.6 4.0 %copy-start.85 = (f32[5,128]{1,0:T(8,128)S(1)}, f32[5,128]{1,0:T(8,128)}, u32[]{:S(2)}) copy-start(f32[5,128]{1,0:T(8,128)} %get-tuple-element.65) | copy-start | bytes 7684
  217.6 34.2 %all-to-all-start.7 = ((bf16[8,32,2560]{2,1,0:T(8,128)(2,1)}), bf16[8,32,2560]{2,1,0:T(8,128)(2,1)S(1)}, u32[]{:S(2)}, u32[]{:S(2)}) async-start(bf16[8,32,2560]{2,1,0:T(8,128)(2,1)} %convert_element_type.150), calls=%async_computation.7 | async-start | bytes 2621440 | tf_op jit(solution)/shard_map/all_to_all | solution.py:194
  229.3 5.2 %copy-start.25 = (bf16[5,256,128]{1,2,0:T(8,128)(2,1)S(1)}, bf16[5,256,128]{1,2,0:T(8,128)(2,1)}, u32[]{:S(2)}) copy-start(bf16[5,256,128]{1,2,0:T(8,128)(2,1)} %copy-done.24) | copy-start | bytes 983044
  (51 other events, 102.2 us)
where the time goes:
time: 256 us; the launch traced here: 254 us
  waiting for transfers between devices  88.5 us (35%)
  local copies, waits for them, and re-layouts  73.6 us (29%)
  starting transfers between devices  35.4 us (14%)
  matrix products  35.3 us (14%)
  other arithmetic  18.9 us (7%)
    all_to_all x1, waiting for transfers between devices, per_device(): lax.all_to_all(to_slots(queries), 'wide', split_axis=0, concat_axis=0, ti...  31.4 us
    all_to_all x1, waiting for transfers between devices, per_device(): lax.all_to_all(prefix_out, 'wide', split_axis=0, concat_axis=0, tiled=True)  16.1 us
    unnamed x200, local copies, waits for them, and re-layouts  15.8 us
    all_to_all x1, waiting for transfers between devices, per_device(): lax.all_to_all(prefix_query.astype(jnp.bfloat16), 'wide', split_axis=0, c...  15.2 us
    all_to_all x1, waiting for transfers between devices, per_device(): lax.all_to_all(to_slots(out_grad).astype(jnp.float32), 'wide', split_axis...  11.7 us
    dot_general x8, matrix products, part_backward(): jnp.einsum('hrk,rhd->kd', dscore, query_block, preferred_element_type=jnp...  9.27 us
    scatter x4, local copies, waits for them, and re-layouts, to_slots(): return jnp.zeros((slot_total,) + row_array.shape[1:], row_array.dtype).at...  8.73 us
    dot_general x8, matrix products, part_backward(): jnp.einsum('hrk,rhd->kd', probs.astype(jnp.bfloat16), grad_block, preferr...  8.72 us
  transfers between devices with their start and end apart: 8, of which 7 were waited for; matrix products, arithmetic and copies ran while one was open for 33% of the time, Pallas kernels for 0%

commit v1 on v0

v1 whole, which is shorter than its diff:
```python
import functools

import jax
import jax.numpy as jnp
from jax import lax
from jax.experimental import pallas as pl
from jax.experimental.pallas import tpu as pltpu
from jax.sharding import PartitionSpec as P

QH = 40
KH = 8
HD = 128
GRP = QH // KH
MASKED = -1e30


def nt(a, b):
    return lax.dot_general(a, b, (((1,), (1,)), ((), ())), preferred_element_type=jnp.float32)


def nn(a, b):
    return lax.dot_general(a, b, (((1,), (0,)), ((), ())), preferred_element_type=jnp.float32)


def tn(a, b):
    return lax.dot_general(a, b, (((0,), (0,)), ((), ())), preferred_element_type=jnp.float32)


def row_slots(prompt, n_wide, capacity):
    rows = prompt.shape[0]
    lanes = max(128, n_wide)
    hits = prompt == lax.broadcasted_iota(jnp.int32, (rows, lanes), 1)
    earlier = lax.broadcasted_iota(jnp.int32, (rows, rows), 1) < lax.broadcasted_iota(
        jnp.int32, (rows, rows), 0
    )
    seen = nn(
        jnp.where(earlier, 1.0, 0.0).astype(jnp.bfloat16),
        jnp.where(hits, 1.0, 0.0).astype(jnp.bfloat16),
    )
    rank = jnp.sum(jnp.where(hits, seen, 0.0), axis=1, keepdims=True)
    slot = prompt.astype(jnp.float32) * capacity + rank
    places = lax.broadcasted_iota(jnp.int32, (rows, n_wide * capacity), 1).astype(jnp.float32)
    return jnp.where(slot == places, 1.0, 0.0).astype(jnp.bfloat16)


def key_mask(keys, slots, capacity, prefix_rows, bunch):
    shape = (keys, GRP * slots)
    key = lax.broadcasted_iota(jnp.int32, shape, 0)
    row = lax.broadcasted_iota(jnp.int32, shape, 1) % slots
    own = key - bunch * prefix_rows
    same = jnp.where(own >= 0, own // capacity, key // prefix_rows) == row // capacity
    return same & (own <= row)


def attend(q, g, k, v, mask, masked_rows, scale):
    keys = k.shape[0]
    scores = nt(k, q) * scale
    if masked_rows == keys:
        scores = jnp.where(mask, scores, MASKED)
    else:
        scores = jnp.concatenate(
            [
                scores[: keys - masked_rows],
                jnp.where(mask[keys - masked_rows :], scores[keys - masked_rows :], MASKED),
            ],
            axis=0,
        )
    weights = jnp.exp(scores - jnp.max(scores, axis=0, keepdims=True))
    probs = weights * (1.0 / jnp.sum(weights, axis=0, keepdims=True))
    low = probs.astype(jnp.bfloat16)
    dprob = nt(v, g)
    weighted = probs * dprob
    delta = jnp.sum(weighted, axis=0, keepdims=True)
    dscore = (weighted - probs * delta).astype(jnp.bfloat16)
    return tn(low, v), tn(dscore, k) * scale, nn(dscore, q) * scale, nn(low, g)


def group_step(n_wide, capacity, slots, select, q, g, k, v, prefix_of, o_ref, dq_ref, dk_ref, dv_ref, put_prefix):
    scale = HD ** (-0.5)
    bunch = slots // capacity
    tiles = n_wide * capacity // slots
    bf = jnp.bfloat16
    qs, gs, ks, vs = (tn(select, x).astype(bf) for x in (q, g, k, v))
    outs, dqs, dks, dvs = [], [], [], []
    for t in range(tiles):
        span = slice(t * slots, (t + 1) * slots)
        pk, pv = prefix_of(t * bunch, bunch)
        prefix_rows = pk.shape[0] // bunch
        stack = lambda x: jnp.concatenate(
            [x[span, h * HD : (h + 1) * HD] for h in range(GRP)], axis=0
        )
        key_block = jnp.concatenate([pk, ks[span]], axis=0)
        value_block = jnp.concatenate([pv, vs[span]], axis=0)
        keys = key_block.shape[0]
        mask = key_mask(keys, slots, capacity, prefix_rows, bunch)
        out, dq, dk, dv = attend(
            stack(qs), stack(gs), key_block, value_block, mask, slots if bunch == 1 else keys, scale
        )
        unstack = lambda x: jnp.concatenate(
            [x[h * slots : (h + 1) * slots] for h in range(GRP)], axis=1
        ).astype(bf)
        outs.append(unstack(out))
        dqs.append(unstack(dq))
        split = bunch * prefix_rows
        put_prefix(t * bunch, bunch, dk[:split].astype(bf), dv[:split].astype(bf))
        dks.append(dk[split:].astype(bf))
        dvs.append(dv[split:].astype(bf))
    for ref, parts in ((o_ref, outs), (dq_ref, dqs), (dk_ref, dks), (dv_ref, dvs)):
        ref[...] = nn(select, jnp.concatenate(parts, axis=0)).astype(bf)


def kernel(n_wide, capacity, slots, prompt, q, g, k, v, pk, pv, o, dq, dk, dv, pdk, pdv, select):
    @pl.when(pl.program_id(0) == 0)
    def _():
        select[...] = row_slots(prompt[...], n_wide, capacity)

    prefix_rows = pk.shape[0] // n_wide

    def prefix_of(first, count):
        span = pl.ds(first * prefix_rows, count * prefix_rows)
        return pk[span, :], pv[span, :]

    def put_prefix(first, count, dkey, dvalue):
        span = pl.ds(first * prefix_rows, count * prefix_rows)
        pdk[span, :] = dkey
        pdv[span, :] = dvalue

    group_step(
        n_wide, capacity, slots, select[...], q[...], g[...], k[...], v[...], prefix_of, o, dq, dk, dv, put_prefix
    )


def per_device(queries, keys, values, prefix_keys, prefix_values, out_grad, row_prompt):
    n_wide = lax.axis_size("wide")
    rows = queries.shape[0]
    capacity = 2 * rows // n_wide
    slots = max(32, capacity)
    groups = keys.shape[1] // HD
    gather = lambda x: lax.all_gather(x, "wide", axis=0, tiled=True)
    pk, pv = gather(prefix_keys), gather(prefix_values)
    wide_rows = pk.shape[0]
    col = lambda r, c: pl.BlockSpec((r, c), lambda i: (0, i))
    shape = lambda x: jax.ShapeDtypeStruct(x.shape, jnp.bfloat16)
    o, dq, dk, dv, pdk, pdv = pl.pallas_call(
        functools.partial(kernel, n_wide, capacity, slots),
        grid=(groups,),
        out_shape=[shape(x) for x in (queries, queries, keys, values, pk, pv)],
        in_specs=[
            pl.BlockSpec((rows, 1), lambda i: (0, 0)),
            col(rows, GRP * HD),
            col(rows, GRP * HD),
            col(rows, HD),
            col(rows, HD),
            col(wide_rows, HD),
            col(wide_rows, HD),
        ],
        out_specs=[
            col(rows, GRP * HD),
            col(rows, GRP * HD),
            col(rows, HD),
            col(rows, HD),
            col(wide_rows, HD),
            col(wide_rows, HD),
        ],
        scratch_shapes=[pltpu.VMEM((rows, n_wide * capacity), jnp.bfloat16)],
    )(row_prompt, queries, out_grad, keys, values, pk, pv)
    scatter = lambda x: lax.psum_scatter(x, "wide", scatter_dimension=0, tiled=True)
    return o, dq, dk, dv, scatter(pdk), scatter(pdv)


def solution(mesh):
    rows = P(("groups", "wide"), "mp")
    return jax.shard_map(
        per_device,
        mesh=mesh,
        in_specs=(rows,) * 6 + (P(("groups", "wide"), None),),
        out_specs=(rows,) * 6,
        check_vma=False,
    )
```

time: 256 us -> 248 us (0.969)
  waiting for transfers between devices: 88.5 us -> 216 us
  local copies, waits for them, and re-layouts: 73.6 us -> 0.75 us
  matrix products: 35.3 us -> 0 us
  starting transfers between devices: 35.4 us -> 0.15 us
  other arithmetic: 18.9 us -> 0 us
  Pallas kernels: 0 us -> 17.3 us
  between operations: 2.18 us -> 13.8 us
    reduce_scatter x0 -> x2, waiting for transfers between devices: none -> 129 us  [per_device(): lax.psum_scatter(x, 'wide', scatter_dimension=0, tiled=True)]
    all_to_all x8 -> x0, waiting for transfers between devices: 88.5 us -> none  [the longest x1 31.4 us: per_device(): lax.all_to_all(to_slots(queries), 'wide', split_axis=0, concat_axis=0, ti...]
    all_gather x0 -> x2, waiting for transfers between devices: none -> 84.8 us  [per_device(): gather = lambda x: lax.all_gather(x, 'wide', axis=0, tiled=True)]
    all_to_all x8 -> x0, starting transfers between devices: 35.4 us -> none  [the longest x1 7.41 us: per_device(): lax.all_to_all(to_slots(queries), 'wide', split_axis=0, concat_axis=0, ti...]
    dot_general x49 -> x0, matrix products: 35.3 us -> none  [the longest x8 9.27 us: part_backward(): jnp.einsum('hrk,rhd->kd', dscore, query_block, preferred_element_type=jnp...]
    pallas_call x0 -> x1, Pallas kernels: none -> 17.3 us  [per_device(): pl.pallas_call(functools.partial(kernel, n_wide, capacity, slots), grid=(...]
    unnamed x200 -> x3, local copies, waits for them, and re-layouts: 15.8 us -> 0.75 us
    mul x5 -> x0, local copies, waits for them, and re-layouts: 9.41 us -> none  [the longest x2 3.96 us: merge_parts(): second_out.reshape(row_count, head_count, head_size)]
  transfers between devices with their start and end apart: 8 -> 4, of which waited for: 7 -> 4; matrix products, arithmetic and copies ran while one was open for 33% -> 0% of each run, Pallas kernels for 0% -> 0%
where the time goes in v1:
time: 248 us
  waiting for transfers between devices  216 us (87%)
  Pallas kernels  17.3 us (7%)
  between operations  13.8 us (6%)
    reduce_scatter x2, waiting for transfers between devices, per_device(): lax.psum_scatter(x, 'wide', scatter_dimension=0, tiled=True)  129 us
    all_gather x2, waiting for transfers between devices, per_device(): gather = lambda x: lax.all_gather(x, 'wide', axis=0, tiled=True)  84.8 us
    pallas_call x1, Pallas kernels, per_device(): pl.pallas_call(functools.partial(kernel, n_wide, capacity, slots), grid=(...  17.3 us
  transfers between devices with their start and end apart: 4, of which 4 were waited for; matrix products, arithmetic and copies ran while one was open for 0% of the time, Pallas kernels for 0%

profile of v1, /device:TPU:0, one launch (start us, length us, event | category | flops | bytes accessed | tf_op | source)
XLA Modules:
  0.0 248.1 jit_solution(1968741411886646987)
XLA Ops:
  7.2 0.0 all-gather.3.cloned.1.call-start
  7.2 0.7 all-gather.3.cloned.1.call-update
  7.9 0.0 copy-start
  7.9 0.0 all-gather.5.cloned.1.call-start
  8.0 0.7 all-gather.5.cloned.1.call-update
  8.7 0.0 reduce-scatter.3.cloned.1.call-start
  8.7 0.0 copy-done
  8.7 0.7 copy.13.prompt
  9.5 43.7 %all-gather.3.cloned.1.call-done.pk = bf16[1024,512]{1,0:T(8,128)(2,1)} async-done(((bf16[128,512]{1,0:T(8,128)(2,1)}), bf16[1024,512]{1,0:T(8,128)(2,1)}) %all-gather.3.cloned.1.call-update) | async-done | bytes 1048592 | tf_op jit(solution)/shard_map/all_gather | solution.py:139
  53.1 41.1 %all-gather.5.cloned.1.call-done.pv = bf16[1024,512]{1,0:T(8,128)(2,1)} async-done(((bf16[128,512]{1,0:T(8,128)(2,1)}), bf16[1024,512]{1,0:T(8,128)(2,1)}) %all-gather.5.cloned.1.call-update) | async-done | bytes 1048592 | tf_op jit(solution)/shard_map/all_gather | solution.py:139
  94.3 17.3 %shard_map.118 = (bf16[128,2560]{1,0:T(8,128)(2,1)}, bf16[128,2560]{1,0:T(8,128)(2,1)}, bf16[128,512]{1,0:T(8,128)(2,1)}, bf16[128,512]{1,0:T(8,128)(2,1)}, bf16...) custom-call(s32[128,1]{1,0:T(8,128)} %copy.13.prompt, bf16[128,2560]{1,0:T(8,128)(2,1)} %q.1, bf16[128,2560]{1,0:T(8,128)(2,1)} %g.1, ...), custom_call_target="tpu_custom_call" | custom-call | tf_op jit(solution)/shard_map/pallas_call | solution.py:144
  111.6 0.0 reduce-scatter.3.cloned.1.call-update
  111.6 0.0 reduce-scatter.5.cloned.1.call-start
  111.7 0.5 reduce-scatter.5.cloned.1.call-update
  112.2 62.4 %reduce-scatter.3.cloned.1.call-done = bf16[128,512]{1,0:T(8,128)(2,1)} async-done(((bf16[1024,512]{1,0:T(8,128)(2,1)}), bf16[128,512]{1,0:T(8,128)(2,1)}) %reduce-scatter.3.cloned.1.call-update) | async-done | bytes 131088 | tf_op jit(solution)/shard_map/reduce_scatter | solution.py:167
  174.6 67.0 %reduce-scatter.5.cloned.1.call-done = bf16[128,512]{1,0:T(8,128)(2,1)} async-done(((bf16[1024,512]{1,0:T(8,128)(2,1)}), bf16[128,512]{1,0:T(8,128)(2,1)}) %reduce-scatter.5.cloned.1.call-update) | async-done | bytes 131088 | tf_op jit(solution)/shard_map/reduce_scatter | solution.py:167
Async XLA Ops:
  7.2 46.0 %all-gather.3.cloned.1.call-start = ((), (), s32[]{:S(2)}) async-start(), calls=%async_computation.2 | async-start | bytes 1179648 | tf_op jit(solution)/shard_map/all_gather | solution.py:139
  7.9 0.8 copy-start
  7.9 86.4 %all-gather.5.cloned.1.call-start = ((), (), s32[]{:S(2)}) async-start(), calls=%async_computation.3 | async-start | bytes 1179648 | tf_op jit(solution)/shard_map/all_gather | solution.py:139
  8.7 165.9 %reduce-scatter.3.cloned.1.call-start = ((), (), s32[]{:S(2)}) async-start(), calls=%async_computation.4 | async-start | bytes 1179648 | tf_op jit(solution)/shard_map/reduce_scatter | solution.py:167
  111.6 130.0 %reduce-scatter.5.cloned.1.call-start = ((), (), s32[]{:S(2)}) async-start(), calls=%async_computation.5 | async-start | bytes 1179648 | tf_op jit(solution)/shard_map/reduce_scatter | solution.py:167
Sparse Core Ops, SparseCore 0:
  10.1 42.9 all-gather.2
  55.3 38.9 all-gather.4
  111.8 62.8 reduce-scatter.2
  178.4 63.1 reduce-scatter.4

commit v2 on v1

v2 whole, which is shorter than its diff:
```python
import functools

import jax
import jax.numpy as jnp
from jax import lax
from jax.experimental import pallas as pl
from jax.experimental.pallas import tpu as pltpu
from jax.sharding import PartitionSpec as P

QH = 40
KH = 8
HD = 128
GRP = QH // KH
MASKED = -1e30


def nt(a, b):
    return lax.dot_general(a, b, (((1,), (1,)), ((), ())), preferred_element_type=jnp.float32)


def nn(a, b):
    return lax.dot_general(a, b, (((1,), (0,)), ((), ())), preferred_element_type=jnp.float32)


def tn(a, b):
    return lax.dot_general(a, b, (((0,), (0,)), ((), ())), preferred_element_type=jnp.float32)


def row_slots(prompt, n_wide, capacity):
    rows = prompt.shape[0]
    lanes = max(128, n_wide)
    hits = prompt == lax.broadcasted_iota(jnp.int32, (rows, lanes), 1)
    earlier = lax.broadcasted_iota(jnp.int32, (rows, rows), 1) < lax.broadcasted_iota(
        jnp.int32, (rows, rows), 0
    )
    seen = nn(
        jnp.where(earlier, 1.0, 0.0).astype(jnp.bfloat16),
        jnp.where(hits, 1.0, 0.0).astype(jnp.bfloat16),
    )
    rank = jnp.sum(jnp.where(hits, seen, 0.0), axis=1, keepdims=True)
    slot = prompt.astype(jnp.float32) * capacity + rank
    places = lax.broadcasted_iota(jnp.int32, (rows, n_wide * capacity), 1).astype(jnp.float32)
    return jnp.where(slot == places, 1.0, 0.0).astype(jnp.bfloat16)


def key_mask(keys, slots, capacity, prefix_rows, bunch):
    shape = (keys, GRP * slots)
    key = lax.broadcasted_iota(jnp.int32, shape, 0)
    row = lax.broadcasted_iota(jnp.int32, shape, 1) % slots
    own = key - bunch * prefix_rows
    same = jnp.where(own >= 0, own // capacity, key // prefix_rows) == row // capacity
    return same & (own <= row)


def attend(q, g, k, v, mask, masked_rows, scale):
    keys = k.shape[0]
    scores = nt(k, q) * scale
    if masked_rows == keys:
        scores = jnp.where(mask, scores, MASKED)
    else:
        scores = jnp.concatenate(
            [
                scores[: keys - masked_rows],
                jnp.where(mask[keys - masked_rows :], scores[keys - masked_rows :], MASKED),
            ],
            axis=0,
        )
    weights = jnp.exp(scores - jnp.max(scores, axis=0, keepdims=True))
    probs = weights * (1.0 / jnp.sum(weights, axis=0, keepdims=True))
    low = probs.astype(jnp.bfloat16)
    dprob = nt(v, g)
    weighted = probs * dprob
    delta = jnp.sum(weighted, axis=0, keepdims=True)
    dscore = (weighted - probs * delta).astype(jnp.bfloat16)
    return tn(low, v), tn(dscore, k) * scale, nn(dscore, q) * scale, nn(low, g)


def ring_index(position, count):
    half = count // 2
    position = lax.rem(position + 2 * count, count)
    return jnp.where(position < half, 2 * position, 2 * (count - 1 - position) + 1)


def ring_position(index, count):
    return jnp.where(index % 2 == 0, index // 2, count - 1 - index // 2)


def kernel(
    n, capacity, slots, groups,
    prompt, q, g, k, v, pk, pv, o, dq, dk, dv, pdk, pdv,
    kv, part, landed, qs, gs, ks, vs, os, dqs, dks, dvs,
    own_sem, ag_send, ag_recv, rs_send, rs_recv,
):
    bf = jnp.bfloat16
    scale = HD ** (-0.5)
    half = n // 2
    bunch = slots // capacity
    tiles = n * capacity // slots
    rows = pk.shape[0]
    width = GRP * HD
    me = lax.axis_index("wide")
    here = ring_position(me, n)
    at = lambda offset: ring_index(here + offset, n)
    right, left = at(1), at(-1)
    copies = []

    own = []
    for c in range(groups):
        for part_id, ref in enumerate((pk, pv)):
            copy = pltpu.make_async_copy(
                ref.at[:, pl.ds(c * HD, HD)],
                kv.at[me, c, pl.ds(part_id * rows, rows)],
                own_sem.at[c, part_id],
            )
            copy.start()
            own.append(copy)

    barrier = pltpu.get_barrier_semaphore()
    for other in (left, right):
        pl.semaphore_signal(
            barrier, inc=1, device_id={"wide": other}, device_id_type=pl.DeviceIdType.MESH
        )
    pl.semaphore_wait(barrier, 2)

    def send(src, dst, send_sem, recv_sem, device):
        return pltpu.make_async_remote_copy(
            src_ref=src,
            dst_ref=dst,
            send_sem=send_sem,
            recv_sem=recv_sem,
            device_id={"wide": device},
            device_id_type=pl.DeviceIdType.MESH,
        )

    def span(way, short):
        return pl.ds(way * rows, rows) if short else pl.ds(0, 2 * rows)

    def gather_copy(way, c, s):
        sign = 1 - 2 * way
        block = kv.at[at(-sign * (s - 1)), c, span(way, s == half)]
        return send(
            block, block, ag_send.at[way, c, s - 1], ag_recv.at[way, c, s - 1], (right, left)[way]
        )

    def gather(c, s):
        if s == 0:
            own[2 * c].wait()
            own[2 * c + 1].wait()
        for way in range(2):
            if s > 0:
                gather_copy(way, c, s).wait_recv()
            if s < half:
                copy = gather_copy(way, c, s + 1)
                copy.start()
                copies.append(copy)

    def reduce_copy(way, c, s):
        sign = 1 - 2 * way
        part_of = span(way, s == 1)
        return send(
            part.at[at(sign * (half + 1 - s)), c, part_of],
            landed.at[way, c, s - 1, part_of],
            rs_send.at[way, c, s - 1],
            rs_recv.at[way, c, s - 1],
            (right, left)[way],
        )

    def reduce(c, s):
        for way in range(2):
            sign = 1 - 2 * way
            if s > 1:
                reduce_copy(way, c, s - 1).wait_recv()
            if s <= half:
                if s > 1:
                    part_of = span(way, s == 2)
                    target = at(sign * (half + 1 - s))
                    part[target, c, part_of] = (
                        part[target, c, part_of].astype(jnp.float32)
                        + landed[way, c, s - 2, part_of].astype(jnp.float32)
                    ).astype(bf)
                copy = reduce_copy(way, c, s)
                copy.start()
                copies.append(copy)
        if s > half:
            for part_id, ref in enumerate((pdk, pdv)):
                part_of = pl.ds(part_id * rows, rows)
                total = part[me, c, part_of].astype(jnp.float32)
                for way in range(2):
                    if half > 1 or way == part_id:
                        total += landed[way, c, half - 1, part_of].astype(jnp.float32)
                ref[:, pl.ds(c * HD, HD)] = total.astype(bf)

    waits = sorted((c + s, c, s) for c in range(groups) for s in range(half + 1))
    for tick, c, s in [w for w in waits if w[0] < 2]:
        gather(c, s)
    waits = [w for w in waits if w[0] >= 2]

    select = row_slots(prompt[...], n, capacity)
    for src, dst in ((k, ks), (v, vs)):
        dst[...] = tn(select, src[...]).astype(bf)

    def to_slots(c):
        for src, dst in ((q, qs), (g, gs)):
            dst[:, c * width : (c + 1) * width] = tn(select, src[:, c * width : (c + 1) * width]).astype(bf)

    to_slots(0)
    ready = 1

    def from_slots(c):
        for slot_ref, ref, cols in ((os, o, width), (dqs, dq, width), (dks, dk, HD), (dvs, dv, HD)):
            ref[:, c * cols : (c + 1) * cols] = nn(select, slot_ref[...]).astype(bf)

    keys = bunch * rows + slots
    mask = key_mask(keys, slots, capacity, rows, bunch)
    ahead = [half]
    for step in range(half - 1, 0, -1):
        ahead += [step, -step]
    ahead += [0]

    def tile(c, t):
        first = at(ahead[t]) if bunch == 1 else t * bunch
        place = pl.ds(pl.multiple_of(first * capacity, slots), slots)
        stack = lambda ref: jnp.concatenate(
            [ref[place, c * width + h * HD : c * width + (h + 1) * HD] for h in range(GRP)], axis=0
        )
        cols = slice(c * HD, (c + 1) * HD)
        key_block = jnp.concatenate(
            [kv[first + i, c, :rows] for i in range(bunch)] + [ks[place, cols]], axis=0
        )
        value_block = jnp.concatenate(
            [kv[first + i, c, rows:] for i in range(bunch)] + [vs[place, cols]], axis=0
        )
        out, dquery, dkey, dvalue = attend(
            stack(qs), stack(gs), key_block, value_block, mask, slots if bunch == 1 else keys, scale
        )
        for ref, value in ((os, out), (dqs, dquery)):
            for h in range(GRP):
                ref[place, h * HD : (h + 1) * HD] = value[h * slots : (h + 1) * slots].astype(bf)
        for i in range(bunch):
            piece = slice(i * rows, (i + 1) * rows)
            part[first + i, c, :rows] = dkey[piece].astype(bf)
            part[first + i, c, rows:] = dvalue[piece].astype(bf)
        dks[place, :] = dkey[bunch * rows :].astype(bf)
        dvs[place, :] = dvalue[bunch * rows :].astype(bf)

    reduces = []
    for c in range(groups):
        reduces.append((c * tiles + (0 if bunch == 1 else tiles - 1), c, 1))
        for s in range(2, half + 2):
            reduces.append((c * tiles + tiles - 1 + 5 * (s - 2), c, s))
    reduces.sort()

    for c in range(groups):
        while waits and waits[0][:2] <= (half + c, c):
            tick, other, s = waits.pop(0)
            gather(other, s)
            if ready < groups:
                to_slots(ready)
                ready += 1
        while ready < min(groups, c + 2):
            to_slots(ready)
            ready += 1
        for t in range(tiles):
            tile(c, t)
            if t % 2 == 0 and waits and waits[0][0] <= half + c:
                tick, other, s = waits.pop(0)
                gather(other, s)
            while reduces and reduces[0][0] <= c * tiles + t:
                _, other, s = reduces.pop(0)
                reduce(other, s)
        from_slots(c)
    for _, other, s in reduces:
        reduce(other, s)
    for copy in copies:
        copy.wait_send()


def per_device(queries, keys, values, prefix_keys, prefix_values, out_grad, row_prompt):
    n = lax.axis_size("wide")
    rows = queries.shape[0]
    prefix_rows = prefix_keys.shape[0]
    capacity = 2 * rows // n
    slots = max(32, capacity)
    places = n * capacity
    groups = keys.shape[1] // HD
    half = n // 2
    bf = jnp.bfloat16
    shape = lambda x: jax.ShapeDtypeStruct(x.shape, bf)
    vmem = pl.BlockSpec(memory_space=pltpu.VMEM)
    anywhere = pl.BlockSpec(memory_space=pl.ANY)
    sems = pltpu.SemaphoreType.DMA
    return pl.pallas_call(
        functools.partial(kernel, n, capacity, slots, groups),
        out_shape=[shape(x) for x in (queries, queries, keys, values, prefix_keys, prefix_values)],
        in_specs=[vmem] * 5 + [anywhere] * 2,
        out_specs=[vmem] * 6,
        scratch_shapes=[
            pltpu.VMEM((n, groups, 2 * prefix_rows, HD), bf),
            pltpu.VMEM((n, groups, 2 * prefix_rows, HD), bf),
            pltpu.VMEM((2, groups, half, 2 * prefix_rows, HD), bf),
            pltpu.VMEM((places, queries.shape[1]), bf),
            pltpu.VMEM((places, queries.shape[1]), bf),
            pltpu.VMEM((places, keys.shape[1]), bf),
            pltpu.VMEM((places, keys.shape[1]), bf),
            pltpu.VMEM((places, GRP * HD), bf),
            pltpu.VMEM((places, GRP * HD), bf),
            pltpu.VMEM((places, HD), bf),
            pltpu.VMEM((places, HD), bf),
            sems((groups, 2)),
            sems((2, groups, half)),
            sems((2, groups, half)),
            sems((2, groups, half)),
            sems((2, groups, half)),
        ],
        compiler_params=pltpu.CompilerParams(collective_id=0, has_side_effects=True),
    )(row_prompt, queries, out_grad, keys, values, prefix_keys, prefix_values)


def solution(mesh):
    rows = P(("groups", "wide"), "mp")
    return jax.shard_map(
        per_device,
        mesh=mesh,
        in_specs=(rows,) * 6 + (P(("groups", "wide"), None),),
        out_specs=(rows,) * 6,
        check_vma=False,
    )
```

time: 248 us -> 67.8 us (0.27)
  waiting for transfers between devices: 216 us -> 0 us
  Pallas kernels: 17.3 us -> 58.9 us
  between operations: 13.8 us -> 0.66 us
  local copies, waits for them, and re-layouts: 0.75 us -> 7.95 us
    reduce_scatter x2 -> x0, waiting for transfers between devices: 129 us -> none  [per_device(): lax.psum_scatter(x, 'wide', scatter_dimension=0, tiled=True)]
    all_gather x2 -> x0, waiting for transfers between devices: 84.8 us -> none  [per_device(): gather = lambda x: lax.all_gather(x, 'wide', axis=0, tiled=True)]
    pallas_call x1, Pallas kernels: 17.3 us -> 58.9 us  [per_device(): pl.pallas_call(functools.partial(kernel, n, capacity, slots, groups), out...]
    unnamed x3 -> x17, local copies, waits for them, and re-layouts: 0.75 us -> 7.95 us
  transfers between devices with their start and end apart: 4 -> 0, of which waited for: 4 -> 0; matrix products, arithmetic and copies ran while one was open for 0% -> 0% of each run, Pallas kernels for 0% -> 0%
where the time goes in v2:
time: 67.8 us; the launch traced here: 67.6 us
  Pallas kernels  58.9 us (87%)
  local copies, waits for them, and re-layouts  7.95 us (12%)
    pallas_call x1, Pallas kernels, per_device(): pl.pallas_call(functools.partial(kernel, n, capacity, slots, groups), out...  58.9 us
    unnamed x17, local copies, waits for them, and re-layouts  7.95 us

profile of v2, /device:TPU:0, one launch (start us, length us, event | category | flops | bytes accessed | tf_op | source)
XLA Modules:
  0.0 67.6 jit_solution(18188832448778345446)
XLA Ops:
  0.6 1.4 %copy.13.prompt = s32[128,1]{1,0:T(8,128)} copy(s32[128,1]{0,1:T(1,128)} %param.13) | data formatting | bytes 1024 | tf_op args[6]
  2.0 58.9 %shard_map.118 = (bf16[128,2560]{1,0:T(8,128)(2,1)}, bf16[128,2560]{1,0:T(8,128)(2,1)}, bf16[128,512]{1,0:T(8,128)(2,1)}, bf16[128,512]{1,0:T(8,128)(2,1)}, bf16...) custom-call(s32[128,1]{1,0:T(8,128)} %copy.13.prompt, bf16[128,2560]{1,0:T(8,128)(2,1)} %q.1, bf16[128,2560]{1,0:T(8,128)(2,1)} %g.1, ...), custom_call_target="tpu_custom_call" | custom-call | tf_op jit(solution)/shard_map/pallas_call | solution.py:292
  61.0 0.0 copy-start
  61.0 2.0 %copy.20 = bf16[128,2560]{1,0:T(8,128)(2,1)} copy(bf16[128,2560]{1,0:T(8,128)(2,1)} %get-tuple-element.12) | data formatting | bytes 1310720
  63.0 0.0 copy-done
  63.0 0.0 copy-start.4
  63.0 0.8 %copy.21 = bf16[128,2560]{1,0:T(8,128)(2,1)} copy(bf16[128,2560]{1,0:T(8,128)(2,1)S(1)} %copy-done) | data formatting | bytes 1310720
  63.9 0.2 copy-done.4
  64.0 0.0 copy-start.3
  64.0 0.7 copy.22
  64.7 0.3 copy-done.3
  65.0 0.0 copy-start.2
  65.0 0.7 copy.23
  65.7 0.3 copy-done.2
  65.9 0.0 copy-start.1
  66.0 0.7 copy.24
  66.6 0.3 copy-done.1
  66.9 0.7 copy.25
Async XLA Ops:
  61.0 2.0 %copy-start = (bf16[128,2560]{1,0:T(8,128)(2,1)S(1)}, bf16[128,2560]{1,0:T(8,128)(2,1)}, u32[]{:S(2)}) copy-start(bf16[128,2560]{1,0:T(8,128)(2,1)} %get-tuple-element.13) | copy-start | bytes 1966084
  63.0 1.0 %copy-start.4 = (bf16[128,512]{1,0:T(8,128)(2,1)S(1)}, bf16[128,512]{1,0:T(8,128)(2,1)}, u32[]{:S(2)}) copy-start(bf16[128,512]{1,0:T(8,128)(2,1)} %get-tuple-element.14) | copy-start | bytes 393220
  64.0 1.0 %copy-start.3 = (bf16[128,512]{1,0:T(8,128)(2,1)S(1)}, bf16[128,512]{1,0:T(8,128)(2,1)}, u32[]{:S(2)}) copy-start(bf16[128,512]{1,0:T(8,128)(2,1)} %get-tuple-element.15) | copy-start | bytes 393220
  65.0 1.0 %copy-start.2 = (bf16[128,512]{1,0:T(8,128)(2,1)S(1)}, bf16[128,512]{1,0:T(8,128)(2,1)}, u32[]{:S(2)}) copy-start(bf16[128,512]{1,0:T(8,128)(2,1)} %get-tuple-element.16) | copy-start | bytes 393220
  65.9 1.0 %copy-start.1 = (bf16[128,512]{1,0:T(8,128)(2,1)S(1)}, bf16[128,512]{1,0:T(8,128)(2,1)}, u32[]{:S(2)}) copy-start(bf16[128,512]{1,0:T(8,128)(2,1)} %get-tuple-element.17) | copy-start | bytes 393220

commit v3 on v2

--- a/solution.py
+++ b/solution.py
@@ -12,6 +12,9 @@
 HD = 128
 GRP = QH // KH
 MASKED = -1e30
+LEAD = 2
+EARLY = 4
+GAP = 12
 
 
 def nt(a, b):
@@ -27,8 +30,9 @@
 
 
 def row_slots(prompt, n_wide, capacity):
-    rows = prompt.shape[0]
+    rows = prompt.shape[1]
     lanes = max(128, n_wide)
+    prompt = jnp.broadcast_to(prompt.astype(jnp.float32), (128, rows)).T[:, :1].astype(jnp.int32)
     hits = prompt == lax.broadcasted_iota(jnp.int32, (rows, lanes), 1)
     earlier = lax.broadcasted_iota(jnp.int32, (rows, rows), 1) < lax.broadcasted_iota(
         jnp.int32, (rows, rows), 0
@@ -87,9 +91,9 @@
 
 def kernel(
     n, capacity, slots, groups,
-    prompt, q, g, k, v, pk, pv, o, dq, dk, dv, pdk, pdv,
-    kv, part, landed, qs, gs, ks, vs, os, dqs, dks, dvs,
-    own_sem, ag_send, ag_recv, rs_send, rs_recv,
+    prompt, q_far, g_far, k, v, pk, pv, o, dq, dk, dv, pdk, pdv,
+    q, g, kv, part, landed, qs, gs, ks, vs, os, dqs, dks, dvs,
+    in_sem, own_sem, ag_send, ag_recv, rs_send, rs_recv,
 ):
     bf = jnp.bfloat16
     scale = HD ** (-0.5)
@@ -114,6 +118,13 @@
             )
             copy.start()
             own.append(copy)
+
+    loads = [
+        pltpu.make_async_copy(src, dst, in_sem.at[i])
+        for i, (src, dst) in enumerate(((q_far, q), (g_far, g)))
+    ]
+    for copy in loads:
+        copy.start()
 
     barrier = pltpu.get_barrier_semaphore()
     for other in (left, right):
@@ -190,10 +201,11 @@
                         total += landed[way, c, half - 1, part_of].astype(jnp.float32)
                 ref[:, pl.ds(c * HD, HD)] = total.astype(bf)
 
-    waits = sorted((c + s, c, s) for c in range(groups) for s in range(half + 1))
-    for tick, c, s in [w for w in waits if w[0] < 2]:
+    lag = lambda c: max(0, c + 1 - LEAD)
+    waits = sorted((lag(c) + s, c, s) for c in range(groups) for s in range(half + 1))
+    for tick, c, s in [w for w in waits if w[0] == 0]:
         gather(c, s)
-    waits = [w for w in waits if w[0] >= 2]
+    waits = [w for w in waits if w[0] > 0]
 
     select = row_slots(prompt[...], n, capacity)
     for src, dst in ((k, ks), (v, vs)):
@@ -203,8 +215,9 @@
         for src, dst in ((q, qs), (g, gs)):
             dst[:, c * width : (c + 1) * width] = tn(select, src[:, c * width : (c + 1) * width]).astype(bf)
 
-    to_slots(0)
-    ready = 1
+    for copy in loads:
+        copy.wait()
+    ready = 0
 
     def from_slots(c):
         for slot_ref, ref, cols in ((os, o, width), (dqs, dq, width), (dks, dk, HD), (dvs, dv, HD)):
@@ -247,11 +260,12 @@
     for c in range(groups):
         reduces.append((c * tiles + (0 if bunch == 1 else tiles - 1), c, 1))
         for s in range(2, half + 2):
-            reduces.append((c * tiles + tiles - 1 + 5 * (s - 2), c, s))
+            early = EARLY if c == groups - 1 and bunch == 1 else 0
+            reduces.append((c * tiles + tiles - 1 - early + GAP * (s - 2), c, s))
     reduces.sort()
 
     for c in range(groups):
-        while waits and waits[0][:2] <= (half + c, c):
+        while waits and waits[0][:2] <= (half + lag(c), c):
             tick, other, s = waits.pop(0)
             gather(other, s)
             if ready < groups:
@@ -262,7 +276,7 @@
             ready += 1
         for t in range(tiles):
             tile(c, t)
-            if t % 2 == 0 and waits and waits[0][0] <= half + c:
+            if t % 2 == 0 and waits and waits[0][0] <= half + lag(c):
                 tick, other, s = waits.pop(0)
                 gather(other, s)
             while reduces and reduces[0][0] <= c * tiles + t:
@@ -273,6 +287,17 @@
         reduce(other, s)
     for copy in copies:
         copy.wait_send()
+
+
+def write_out(*refs):
+    count = (len(refs) - 1) // 2
+    copies = [
+        pltpu.make_async_copy(refs[i], refs[count + i], refs[-1].at[i]) for i in range(count)
+    ]
+    for copy in copies:
+        copy.start()
+    for copy in copies:
+        copy.wait()
 
 
 def per_device(queries, keys, values, prefix_keys, prefix_values, out_grad, row_prompt):
@@ -289,12 +314,14 @@
     vmem = pl.BlockSpec(memory_space=pltpu.VMEM)
     anywhere = pl.BlockSpec(memory_space=pl.ANY)
     sems = pltpu.SemaphoreType.DMA
-    return pl.pallas_call(
+    results = pl.pallas_call(
         functools.partial(kernel, n, capacity, slots, groups),
         out_shape=[shape(x) for x in (queries, queries, keys, values, prefix_keys, prefix_values)],
-        in_specs=[vmem] * 5 + [anywhere] * 2,
+        in_specs=[vmem] + [anywhere] * 2 + [vmem] * 2 + [anywhere] * 2,
         out_specs=[vmem] * 6,
         scratch_shapes=[
+            pltpu.VMEM(queries.shape, bf),
+            pltpu.VMEM(queries.shape, bf),
             pltpu.VMEM((n, groups, 2 * prefix_rows, HD), bf),
             pltpu.VMEM((n, groups, 2 * prefix_rows, HD), bf),
             pltpu.VMEM((2, groups, half, 2 * prefix_rows, HD), bf),
@@ -306,6 +333,7 @@
             pltpu.VMEM((places, GRP * HD), bf),
             pltpu.VMEM((places, HD), bf),
             pltpu.VMEM((places, HD), bf),
+            sems((2,)),
             sems((groups, 2)),
             sems((2, groups, half)),
             sems((2, groups, half)),
@@ -313,7 +341,14 @@
             sems((2, groups, half)),
         ],
         compiler_params=pltpu.CompilerParams(collective_id=0, has_side_effects=True),
-    )(row_prompt, queries, out_grad, keys, values, prefix_keys, prefix_values)
+    )(row_prompt.T, queries, out_grad, keys, values, prefix_keys, prefix_values)
+    return pl.pallas_call(
+        write_out,
+        out_shape=[shape(x) for x in results],
+        in_specs=[vmem] * len(results),
+        out_specs=[anywhere] * len(results),
+        scratch_shapes=[sems((len(results),))],
+    )(*results)
 
 
 def solution(mesh):

time: 67.8 us -> 58.1 us (0.86)
  local copies, waits for them, and re-layouts: 7.95 us -> 0 us
  Pallas kernels: 58.9 us -> 57.3 us
    unnamed x17 -> x0, local copies, waits for them, and re-layouts: 7.95 us -> none
    pallas_call x1, Pallas kernels: 58.9 us -> 54.6 us  [per_device(): pl.pallas_call(functools.partial(kernel, n, capacity, slots, groups), out...]
    pallas_call x0 -> x1, Pallas kernels: none -> 2.69 us  [per_device(): pl.pallas_call(write_out, out_shape=[shape(x) for x in results], in_specs...]
where the time goes in v3:
time: 58.1 us; the launch traced here: 58 us
  Pallas kernels  57.3 us (99%)
  between operations  0.64 us (1%)
    pallas_call x1, Pallas kernels, per_device(): pl.pallas_call(functools.partial(kernel, n, capacity, slots, groups), out...  54.6 us
    pallas_call x1, Pallas kernels, per_device(): pl.pallas_call(write_out, out_shape=[shape(x) for x in results], in_specs...  2.69 us

profile of v3, /device:TPU:0, one launch (start us, length us, event | category | flops | bytes accessed | tf_op | source)
XLA Modules:
  0.0 58.0 jit_solution(12071344067176153388)
XLA Ops:
  0.6 54.6 %shard_map.118 = (bf16[128,2560]{1,0:T(8,128)(2,1)}, bf16[128,2560]{1,0:T(8,128)(2,1)}, bf16[128,512]{1,0:T(8,128)(2,1)}, bf16[128,512]{1,0:T(8,128)(2,1)}, bf16...) custom-call(s32[1,128]{1,0:T(1,128)} %bitcast.1, bf16[128,2560]{1,0:T(8,128)(2,1)} %q_far.1, bf16[128,2560]{1,0:T(8,128)(2,1)} %g_far.1, ...), custom_call_target="tpu_custom_call" | custom-call | tf_op jit(solution)/shard_map/pallas_call | solution.py:317
  55.3 2.7 %shard_map.119 = (bf16[128,2560]{1,0:T(8,128)(2,1)}, bf16[128,2560]{1,0:T(8,128)(2,1)}, bf16[128,512]{1,0:T(8,128)(2,1)}, bf16[128,512]{1,0:T(8,128)(2,1)}, bf16...) custom-call(bf16[128,2560]{1,0:T(8,128)(2,1)} %get-tuple-element.12.refs_0_, bf16[128,2560]{1,0:T(8,128)(2,1)} %get-tuple-element.13.refs_1_, ...), custom_call_target="tpu_custom_call" | custom-call | tf_op jit(solution)/shard_map/pallas_call | solution.py:345

commit v4 on v3

--- a/solution.py
+++ b/solution.py
@@ -13,8 +13,8 @@
 GRP = QH // KH
 MASKED = -1e30
 LEAD = 2
-EARLY = 4
-GAP = 12
+EARLY = 5
+GAP = 10
 
 
 def nt(a, b):
@@ -290,13 +290,19 @@
 
 
 def write_out(*refs):
-    count = (len(refs) - 1) // 2
-    copies = [
-        pltpu.make_async_copy(refs[i], refs[count + i], refs[-1].at[i]) for i in range(count)
+    count = len(refs) // 3
+    sems = refs[-1]
+    steps = [
+        pltpu.make_async_copy(refs[a * count + i], refs[b * count + i], sems.at[k, i])
+        for k, (a, b) in enumerate(((0, 2), (2, 1)))
+        for i in range(count)
     ]
-    for copy in copies:
+    for copy in steps[:count]:
         copy.start()
-    for copy in copies:
+    for i in range(count):
+        steps[i].wait()
+        steps[count + i].start()
+    for copy in steps[count:]:
         copy.wait()
 
 
@@ -345,9 +351,9 @@
     return pl.pallas_call(
         write_out,
         out_shape=[shape(x) for x in results],
-        in_specs=[vmem] * len(results),
+        in_specs=[anywhere] * len(results),
         out_specs=[anywhere] * len(results),
-        scratch_shapes=[sems((len(results),))],
+        scratch_shapes=[pltpu.VMEM(x.shape, bf) for x in results] + [sems((2, len(results)))],
     )(*results)
 
 

time: 58.1 us -> 57.6 us (level)
  no operation moved by 1% of the time
where the time goes in v4:
time: 57.6 us; the launch traced here: 57.5 us
  Pallas kernels  56.8 us (99%)
  between operations  0.64 us (1%)
    pallas_call x1, Pallas kernels, per_device(): pl.pallas_call(functools.partial(kernel, n, capacity, slots, groups), out...  54.4 us
    pallas_call x1, Pallas kernels, per_device(): pl.pallas_call(write_out, out_shape=[shape(x) for x in results], in_specs...  2.41 us

profile of v4, /device:TPU:0, one launch (start us, length us, event | category | flops | bytes accessed | tf_op | source)
XLA Modules:
  0.0 57.5 jit_solution(3265598205504692828)
XLA Ops:
  0.6 54.4 %shard_map.118 = (bf16[128,2560]{1,0:T(8,128)(2,1)}, bf16[128,2560]{1,0:T(8,128)(2,1)}, bf16[128,512]{1,0:T(8,128)(2,1)}, bf16[128,512]{1,0:T(8,128)(2,1)}, bf16...) custom-call(s32[1,128]{1,0:T(1,128)} %bitcast.1, bf16[128,2560]{1,0:T(8,128)(2,1)} %q_far.1, bf16[128,2560]{1,0:T(8,128)(2,1)} %g_far.1, ...), custom_call_target="tpu_custom_call" | custom-call | tf_op jit(solution)/shard_map/pallas_call | solution.py:323
  55.0 2.4 %shard_map.119 = (bf16[128,2560]{1,0:T(8,128)(2,1)}, bf16[128,2560]{1,0:T(8,128)(2,1)}, bf16[128,512]{1,0:T(8,128)(2,1)}, bf16[128,512]{1,0:T(8,128)(2,1)}, bf16...) custom-call(bf16[128,2560]{1,0:T(8,128)(2,1)} %get-tuple-element.12.refs_0_, bf16[128,2560]{1,0:T(8,128)(2,1)} %get-tuple-element.13.refs_1_, ...), custom_call_target="tpu_custom_call" | custom-call | tf_op jit(solution)/shard_map/pallas_call | solution.py:351
